TPU v7x, 32 devices: a whole 2x2x4 slice. The times are simulated.
32 devices in a mesh: src: 16 (over z, y, core), tgt: 2 (over x).
Axes of the slice: x: 2, y: 2, z: 4, core: 2. Of those that a mesh axis runs over, the one named last changes fastest.
Arguments:
- inputs: bfloat16 [64, 2, 1024, 512], P(('src', 'tgt')), may hold values from -6 to 6
- leaf_maps: bfloat16 [64, 2, 256, 1024], P(('src', 'tgt')), may hold values from -0.125 to 0.125
- transfer_blocks: bfloat16 [4, 64, 2, 2, 256, 256], P(None, ('src', 'tgt')), may hold values from -0.1875 to 0.1875
Outputs:
- butterfly_out: bfloat16 [64, 2, 256, 512], P(('src', 'tgt'))
All inputs are finite; a program needn't handle non-finite values.
Results may differ from a plain program's by a relative error of at most 0.012.
Values may be sent and summed in bfloat16 or wider, within the bound.
A program may use at most 64 MiB of HBM per device.

v0:
```python
import jax
import jax.numpy as jnp
from jax import lax
from jax.sharding import PartitionSpec as P


def partner_2(block, axis, apart):
    count = lax.axis_size(axis)
    route = []
    for low in range(count):
        high = low | 1 << apart
        if high != low and high < count:
            route += [(low, high), (high, low)]
    return lax.ppermute(block, axis, route)


def batched(left_side, right_side):
    return jnp.einsum("nij,njr->nir", left_side, right_side, preferred_element_type=jnp.float32)


def complex_product(blocks, vectors):
    real_part = batched(blocks[:, 0], vectors[:, 0]) - batched(blocks[:, 1], vectors[:, 1])
    imag_part = batched(blocks[:, 0], vectors[:, 1]) + batched(blocks[:, 1], vectors[:, 0])
    return jnp.stack([real_part, imag_part], axis=1)


def remote_term(coeffs, other_blocks, axis_src, bit_place):
    partial_term = complex_product(other_blocks, coeffs).astype(jnp.bfloat16)
    if axis_src:
        arrived = partner_2(partial_term, "src", bit_place)
    else:
        arrived = partner_2(partial_term, "tgt", bit_place)
    return arrived.astype(jnp.float32)


def butterfly_level(coeffs, blocks, axis_src, bit_place):
    device_index = lax.axis_index("src") if axis_src else lax.axis_index("tgt")
    own_bit = device_index // 2**bit_place % 2
    kept_blocks = lax.dynamic_index_in_dim(blocks, own_bit, axis=1, keepdims=False)
    other_blocks = lax.dynamic_index_in_dim(blocks, 1 - own_bit, axis=1, keepdims=False)
    local_term = complex_product(kept_blocks, coeffs)
    return (local_term + remote_term(coeffs, other_blocks, axis_src, bit_place)).astype(
        jnp.bfloat16
    )


def local(inputs, leaf_maps, transfer_blocks):
    coeffs = complex_product(leaf_maps, inputs).astype(jnp.bfloat16)
    first_blocks = transfer_blocks[0]
    halves = []
    for target_bit in range(2):
        other_bit = 1 - target_bit
        own_term = complex_product(
            first_blocks[target_bit : target_bit + 1, target_bit],
            coeffs[target_bit : target_bit + 1],
        )[0]
        partner = complex_product(
            first_blocks[other_bit : other_bit + 1, target_bit], coeffs[other_bit : other_bit + 1]
        )[0].astype(jnp.bfloat16)
        halves.append(own_term + partner.astype(jnp.float32))
    coeffs = jnp.stack(halves, axis=0).astype(jnp.bfloat16)
    src_bits = lax.axis_size("src").bit_length() - 1
    tgt_bits = lax.axis_size("tgt").bit_length() - 1
    coeffs = butterfly_level(coeffs, transfer_blocks[1], True, src_bits - 1)
    coeffs = butterfly_level(coeffs, transfer_blocks[2], True, src_bits - 2)
    return butterfly_level(coeffs, transfer_blocks[3], False, tgt_bits - 1)


def solution(mesh):
    placed = (
        P(("src", "tgt"), None, None, None),
        P(("src", "tgt"), None, None, None),
        P(None, ("src", "tgt"), None, None, None, None),
    )
    return jax.shard_map(
        local,
        mesh=mesh,
        in_specs=placed,
        out_specs=P(("src", "tgt"), None, None, None),
        check_vma=False,
    )
```

profile of v0, /device:TPU:0, one launch (start us, length us, event | category | flops | bytes accessed | tf_op | source)
XLA Modules:
  0.0 129.0 jit_solution(11616204029301806692)
XLA Ops:
  0.0 2.8 %fusion.3 = f32[2,256,512]{2,1,0:T(8,128)S(1)} fusion(bf16[2,2,1024,512]{3,2,1,0:T(8,128)(2,1)} %param.3, bf16[2,2,256,1024]{3,2,1,0:T(8,128)(2,1)} %param.4), kind=kOutput, calls=%fused_computation.6 | convolution fusion | flops 536870912 | bytes 4194304 | tf_op jit(solution)/shard_map/nij,njr->nir/dot_general | solution.py:18
  2.8 0.4 copy-done.17
  3.1 2.1 %fusion.5 = f32[2,256,512]{2,1,0:T(8,128)S(1)} fusion(bf16[2,2,1024,512]{3,2,1,0:T(8,128)(2,1)S(1)} %copy-done.17, bf16[2,2,256,1024]{3,2,1,0:T(8,128)(2,1)} %param.4), kind=kOutput, calls=%fused_computation.8 | convolution fusion | flops 536870912 | bytes 4194304 | tf_op jit(solution)/shard_map/nij,njr->nir/dot_general | solution.py:18
  5.2 0.7 fusion.33
  6.0 0.7 fusion.36
  6.7 1.5 %copy-done = bf16[4,2,2,2,256,256]{5,4,3,2,1,0:T(8,128)(2,1)S(1)} copy-done((bf16[4,2,2,2,256,256]{5,4,3,2,1,0:T(8,128)(2,1)S(1)}, bf16[4,2,2,2,256,256]{5,4,3,2,1,0:T(8,128)(2,1)}, u32[]{:S(2)}) %copy-start) | copy-done | bytes 4194328
  8.1 1.3 %fusion.90 = (bf16[1,2,2,2,256,256]{5,4,3,2,1,0:T(8,128)(2,1)S(1)}, bf16[1,2,2,2,256,256]{5,4,3,2,1,0:T(8,128)(2,1)}, bf16[2,2,2,256,256]{4,3,2,1,0:T(8,128)(2,1)S(1)}, bf16[1,2,2,2,256,256]{5,4,3,2,1,0:T(8,128)(2,1)S(1)}) fusion(bf16[4,2,2,2,256,256]{5,4,3,2,1,0:T(8,128)(2,1)S(1)} %copy-done), kind=kLoop, calls=%fused_computation.158 | loop fusion | bytes 8388608 | tf_op jit(solution)/shard_map/slice | solution.py:66
  9.6 1.1 fusion.89
  10.6 1.1 fusion.87
  11.7 1.1 fusion.84
  12.7 1.1 fusion.82
  13.8 1.1 fusion.88
  14.9 1.1 fusion.86
  16.0 1.1 fusion.85
  17.0 1.1 fusion.83
  18.1 0.9 constant_dynamic-slice_fusion.2
  19.1 0.4 copy-done.11
  22.6 0.3 fusion.81
  22.9 0.3 fusion.80
  23.3 0.3 fusion.44
  23.6 0.3 fusion.43
  24.0 1.1 pad_maximum_fusion
  25.1 4.1 %collective-permute-start = (bf16[2,2,256,512]{3,2,0,1:T(8,128)(2,1)}, bf16[2,2,256,512]{3,2,0,1:T(8,128)(2,1)}, u32[]{:S(2)}, u32[]{:S(2)}) collective-permute-start(bf16[2,2,256,512]{3,2,0,1:T(8,128)(2,1)} %pad_maximum_fusion), channel_id=1, source_target_pairs={{0,16},{16,0},{2,18},{18,2},{4,20},{20,4},{6,22},{22,6},{8,24},{24... | collective-permute-start | bytes 3145736 | tf_op jit(solution)/shard_map/ppermute | solution.py:14
  29.3 0.8 copy-done.16
  30.2 0.3 fusion.79
  30.6 0.3 fusion.26
  30.9 0.3 fusion.78
  31.2 0.3 fusion.25
  31.6 43.5 %collective-permute-done = bf16[2,2,256,512]{3,2,0,1:T(8,128)(2,1)} collective-permute-done((bf16[2,2,256,512]{3,2,0,1:T(8,128)(2,1)}, bf16[2,2,256,512]{3,2,0,1:T(8,128)(2,1)}, u32[]{:S(2)}, u32[]{:S(2)}) %collective-permute-start) | collective-permute-done | bytes 1048608 | tf_op jit(solution)/shard_map/ppermute | solution.py:14
  75.1 1.6 %fusion = bf16[2,2,256,512]{3,2,0,1:T(8,128)(2,1)S(1)} fusion(f32[2,1,256,512]{3,2,0,1:T(8,128)S(1)} %fusion.25, f32[2,1,256,512]{3,2,0,1:T(8,128)S(1)} %fusion.26, bf16[2,2,256,512]{3,2,0,1:T(8,128)(2,1)} %collective-permute-done), kind=kLoop, calls=%fused_computation.1 | loop fusion | flops 2097152 | bytes 4194304 | tf_op jit(solution)/shard_map/convert_element_type | solution.py:42
  77.0 0.3 fusion.70
  77.3 0.3 fusion.42
  77.6 0.3 fusion.41
  78.0 0.8 collective-permute-start.1
  78.9 0.3 fusion.71
  79.2 0.3 fusion.23
  79.8 0.3 fusion.24
  80.1 22.3 %collective-permute-done.1 = bf16[2,2,256,512]{3,2,0,1:T(8,128)(2,1)S(1)} collective-permute-done((bf16[2,2,256,512]{3,2,0,1:T(8,128)(2,1)S(1)}, bf16[2,2,256,512]{3,2,0,1:T(8,128)(2,1)S(1)}, u32[]{:S(2)}, u32[]{:S(2)}) %collective-permute-start.1) | collective-permute-done | bytes 1048608 | tf_op jit(solution)/shard_map/ppermute | solution.py:14
  102.4 0.4 fusion.1
  103.0 0.3 fusion.74
  103.3 0.3 fusion.40
  103.7 0.3 fusion.39
  104.1 1.4 %collective-permute-start.2 = (bf16[2,2,256,512]{3,2,0,1:T(8,128)(2,1)S(1)}, bf16[2,2,256,512]{3,2,0,1:T(8,128)(2,1)S(1)}, u32[]{:S(2)}, u32[]{:S(2)}) collective-permute-start(bf16[2,2,256,512]{3,2,0,1:T(8,128)(2,1)S(1)} %pad_maximum_fusion.2), channel_id=1, source_target_pairs={{0,1},{1,0},{2,3},{3,2},{4,5},{5,4},{6,7},{7,6},{8,9},{9,8},{10,11... | collective-permute-start | bytes 3145736 | tf_op jit(solution)/shard_map/ppermute | solution.py:14
  105.8 0.3 fusion.21
  106.4 0.3 fusion.22
  106.7 20.9 %collective-permute-done.2 = bf16[2,2,256,512]{3,2,0,1:T(8,128)(2,1)S(1)} collective-permute-done((bf16[2,2,256,512]{3,2,0,1:T(8,128)(2,1)S(1)}, bf16[2,2,256,512]{3,2,0,1:T(8,128)(2,1)S(1)}, u32[]{:S(2)}, u32[]{:S(2)}) %collective-permute-start.2) | collective-permute-done | bytes 1048608 | tf_op jit(solution)/shard_map/ppermute | solution.py:14
  127.6 0.4 fusion.2
  128.0 1.0 copy.22
  (59 shorter events, 5.2 us)
Async XLA Ops:
  0.0 3.1 %copy-start.17 = (bf16[2,2,1024,512]{3,2,1,0:T(8,128)(2,1)S(1)}, bf16[2,2,1024,512]{3,2,1,0:T(8,128)(2,1)}, u32[]{:S(2)}) copy-start(bf16[2,2,1024,512]{3,2,1,0:T(8,128)(2,1)} %param.3) | copy-start | bytes 12582916
  3.1 2.1 %copy-start.18 = (bf16[2,2,256,1024]{3,2,1,0:T(8,128)(2,1)S(1)}, bf16[2,2,256,1024]{3,2,1,0:T(8,128)(2,1)}, u32[]{:S(2)}) copy-start(bf16[2,2,256,1024]{3,2,1,0:T(8,128)(2,1)} %param.4) | copy-start | bytes 6291460
  5.9 2.2 %copy-start = (bf16[4,2,2,2,256,256]{5,4,3,2,1,0:T(8,128)(2,1)S(1)}, bf16[4,2,2,2,256,256]{5,4,3,2,1,0:T(8,128)(2,1)}, u32[]{:S(2)}) copy-start(bf16[4,2,2,2,256,256]{5,4,3,2,1,0:T(8,128)(2,1)} %param.5) | copy-start | bytes 12582916
  9.5 5.4 %copy-start.2 = (bf16[1,2,256,256]{3,2,1,0:T(8,128)(2,1)}, bf16[1,2,256,256]{3,2,1,0:T(8,128)(2,1)S(1)}, u32[]{:S(2)}) copy-start(bf16[1,2,256,256]{3,2,1,0:T(8,128)(2,1)S(1)} %get-tuple-element.17) | copy-start | bytes 786436
  9.5 5.3 %copy-start.6 = (bf16[1,2,256,256]{3,2,1,0:T(8,128)(2,1)}, bf16[1,2,256,256]{3,2,1,0:T(8,128)(2,1)S(1)}, u32[]{:S(2)}) copy-start(bf16[1,2,256,256]{3,2,1,0:T(8,128)(2,1)S(1)} %get-tuple-element.19) | copy-start | bytes 786436
  9.6 7.5 %copy-start.4 = (bf16[1,2,256,256]{3,2,1,0:T(8,128)(2,1)}, bf16[1,2,256,256]{3,2,1,0:T(8,128)(2,1)S(1)}, u32[]{:S(2)}) copy-start(bf16[1,2,256,256]{3,2,1,0:T(8,128)(2,1)S(1)} %get-tuple-element.20) | copy-start | bytes 786436
  18.1 0.9 copy-start.3
  18.1 1.3 %copy-start.11 = (f32[512,256]{1,0:T(8,128)S(1)}, f32[512,256]{1,0:T(8,128)}, u32[]{:S(2)}) copy-start(f32[512,256]{1,0:T(8,128)} %fusion.89) | copy-start | bytes 1572868
  18.1 1.6 %copy-start.10 = (f32[512,256]{1,0:T(8,128)S(1)}, f32[512,256]{1,0:T(8,128)}, u32[]{:S(2)}) copy-start(f32[512,256]{1,0:T(8,128)} %fusion.87) | copy-start | bytes 1572868
  19.0 1.1 copy-start.9
  19.0 1.4 %copy-start.8 = (f32[512,256]{1,0:T(8,128)S(1)}, f32[512,256]{1,0:T(8,128)}, u32[]{:S(2)}) copy-start(f32[512,256]{1,0:T(8,128)} %fusion.82) | copy-start | bytes 1572868
  19.4 1.3 copy-start.7
  19.4 1.3 %copy-start.15 = (f32[512,256]{1,0:T(8,128)S(1)}, f32[512,256]{1,0:T(8,128)}, u32[]{:S(2)}) copy-start(f32[512,256]{1,0:T(8,128)} %fusion.88) | copy-start | bytes 1572868
  20.1 1.1 copy-start.14
  20.4 1.1 copy-start.5
  20.4 1.2 copy-start.13
  20.7 1.2 copy-start.12
  23.6 5.5 %copy-start.1 = (bf16[1,2,2,2,256,256]{5,4,3,2,1,0:T(8,128)(2,1)S(1)}, bf16[1,2,2,2,256,256]{5,4,3,2,1,0:T(8,128)(2,1)}, u32[]{:S(2)}) copy-start(bf16[1,2,2,2,256,256]{5,4,3,2,1,0:T(8,128)(2,1)} %get-tuple-element.6) | copy-start | bytes 3145732
  25.1 50.0 %collective-permute-start = (bf16[2,2,256,512]{3,2,0,1:T(8,128)(2,1)}, bf16[2,2,256,512]{3,2,0,1:T(8,128)(2,1)}, u32[]{:S(2)}, u32[]{:S(2)}) collective-permute-start(bf16[2,2,256,512]{3,2,0,1:T(8,128)(2,1)} %pad_maximum_fusion), channel_id=1, source_target_pairs={{0,16},{16,0},{2,18},{18,2},{4,20},{20,4},{6,22},{22,6},{8,24},{24... | collective-permute-start | bytes 3145736 | tf_op jit(solution)/shard_map/ppermute | solution.py:14
  29.1 1.0 copy-start.16
  78.0 24.4 %collective-permute-start.1 = (bf16[2,2,256,512]{3,2,0,1:T(8,128)(2,1)S(1)}, bf16[2,2,256,512]{3,2,0,1:T(8,128)(2,1)S(1)}, u32[]{:S(2)}, u32[]{:S(2)}) collective-permute-start(bf16[2,2,256,512]{3,2,0,1:T(8,128)(2,1)S(1)} %pad_maximum_fusion.1), channel_id=1, source_target_pairs={{0,8},{8,0},{2,10},{10,2},{4,12},{12,4},{6,14},{14,6},{16,24},{24,... | collective-permute-start | bytes 3145736 | tf_op jit(solution)/shard_map/ppermute | solution.py:14
  104.1 23.5 %collective-permute-start.2 = (bf16[2,2,256,512]{3,2,0,1:T(8,128)(2,1)S(1)}, bf16[2,2,256,512]{3,2,0,1:T(8,128)(2,1)S(1)}, u32[]{:S(2)}, u32[]{:S(2)}) collective-permute-start(bf16[2,2,256,512]{3,2,0,1:T(8,128)(2,1)S(1)} %pad_maximum_fusion.2), channel_id=1, source_target_pairs={{0,1},{1,0},{2,3},{3,2},{4,5},{5,4},{6,7},{7,6},{8,9},{9,8},{10,11... | collective-permute-start | bytes 3145736 | tf_op jit(solution)/shard_map/ppermute | solution.py:14
where the time goes:
time: 129 us
  waiting for transfers between devices  86.7 us (67%)
  matrix products  24.4 us (19%)
  local copies, waits for them, and re-layouts  7.26 us (6%)
  starting transfers between devices  6.21 us (5%)
  other arithmetic  4 us (3%)
    ppermute x3, waiting for transfers between devices, partner_2(): return lax.ppermute(block, axis, route)  86.7 us
    dot_general x44, matrix products, batched(): jnp.einsum('nij,njr->nir', left_side, right_side, preferred_element_type=...  24.4 us
    ppermute x3, starting transfers between devices, partner_2(): return lax.ppermute(block, axis, route)  6.21 us
    unnamed x38, local copies, waits for them, and re-layouts  3.6 us
  transfers between devices with their start and end apart: 3, of which 3 were waited for; matrix products, arithmetic and copies ran while one was open for 3% of the time, Pallas kernels for 0%

commit v1 on v0

v1 whole, which is shorter than its diff:
```python
import functools

import jax
import jax.numpy as jnp
from jax import lax
from jax.experimental import pallas as pl
from jax.experimental.pallas import tpu as pltpu
from jax.sharding import PartitionSpec as P

MESH = pl.DeviceIdType.MESH
LANES = 128


def product(blocks, vectors):
    rows = blocks.shape[0] // 2
    width = vectors.shape[1] // 2
    both = jnp.dot(blocks, vectors, preferred_element_type=jnp.float32)
    real_part = both[:rows, :width] - both[rows:, width:]
    imag_part = both[:rows, width:] + both[rows:, :width]
    return jnp.concatenate([real_part, imag_part], axis=1)


def kernel(
    sizes,
    inputs,
    leaf_maps,
    transfer,
    out,
    x_in,
    maps,
    blocks,
    coeffs,
    send1,
    relay_a,
    relay_b,
    recv1,
    send2,
    recv2,
    send3,
    recv3,
    result,
    in_sem,
    maps_sem,
    blocks_sem,
    out_sem,
    s1_sem,
    ra_sem,
    rb_sem,
    fa_sem,
    fb_sem,
    r1_sem,
    s2_sem,
    r2_sem,
    s3_sem,
    r3_sem,
):
    src_bits, tgt_bits, levels, chunks = sizes
    units = 2 * chunks
    src, tgt = lax.axis_index("src"), lax.axis_index("tgt")
    hi, lo = 2 ** (src_bits - 1), 2 ** (src_bits - 2)
    far = 2 ** (tgt_bits - 1)
    bit1, bit2, bit3 = src // hi % 2, src // lo % 2, tgt // far % 2
    flip_lo = src + lo - 2 * lo * bit2
    flip_both = flip_lo + hi - 2 * hi * bit1
    near = (flip_lo, tgt)
    across = (flip_both, tgt)
    side = (src, tgt + far - 2 * far * bit3)
    is_end = bit1 == bit2
    is_mid = bit1 != bit2

    barrier = pltpu.get_barrier_semaphore()
    for peer in (near, across, side):
        pl.semaphore_signal(barrier, inc=1, device_id=peer, device_id_type=MESH)

    def load_in(c, n, part):
        return pltpu.make_async_copy(
            inputs.at[n, part, :, pl.ds(pl.multiple_of(c * LANES, LANES), LANES)],
            x_in.at[c, n, :, pl.ds(part * LANES, LANES)],
            in_sem.at[c, n, part],
        )

    def load_maps(n):
        return pltpu.make_async_copy(leaf_maps.at[n], maps.at[n], maps_sem.at[n])

    def load_blocks(v):
        return pltpu.make_async_copy(transfer.at[v], blocks.at[v], blocks_sem.at[v])

    for n in range(2):
        load_maps(n).start()
        for part in range(2):
            load_in(0, n, part).start()
    load_blocks(0).start()
    load_blocks(1).start()
    for c in range(1, chunks):
        for n in range(2):
            for part in range(2):
                load_in(c, n, part).start()
    for v in range(2, levels):
        load_blocks(v).start()

    def remote(source, target, send_sem, recv_sem, peer):
        return pltpu.make_async_remote_copy(
            src_ref=source,
            dst_ref=target,
            send_sem=send_sem,
            recv_sem=recv_sem,
            device_id=peer,
            device_id_type=MESH,
        )

    def own_a(u):
        return remote(send1.at[u], relay_a.at[u], s1_sem.at[u], ra_sem.at[u], near)

    def own_b(u):
        return remote(send1.at[u], relay_b.at[u], s1_sem.at[u], rb_sem.at[u], across)

    def forward_a(u):
        return remote(relay_a.at[u], recv1.at[u], fa_sem.at[u], r1_sem.at[u], across)

    def forward_b(u):
        return remote(relay_b.at[u], recv1.at[u], fb_sem.at[u], r1_sem.at[u], near)

    def second(u):
        return remote(send2.at[u], recv2.at[u], s2_sem.at[u], r2_sem.at[u], near)

    def third(u):
        return remote(send3.at[u], recv3.at[u], s3_sem.at[u], r3_sem.at[u], side)

    def forward(u):
        own_b(u).wait_recv()
        forward_b(u).start()
        own_a(u).wait_recv()
        forward_a(u).start()

    def store(u, part):
        return pltpu.make_async_copy(
            result.at[u, :, pl.ds(part * LANES, LANES)],
            out.at[u % 2, part, :, pl.ds(pl.multiple_of(u // 2 * LANES, LANES), LANES)],
            out_sem.at[u, part],
        )

    def pre(c):
        vectors = []
        for n in range(2):
            for part in range(2):
                load_in(c, n, part).wait()
            vectors.append(product(maps[n], x_in[c, n]).astype(jnp.bfloat16))

        @pl.when(c == 0)
        def _():
            load_blocks(0).wait()
            load_blocks(1).wait()

        for n in range(2):
            own_term = product(blocks[0, n, n], vectors[n])
            partner = product(blocks[0, 1 - n, n], vectors[1 - n]).astype(jnp.bfloat16)
            updated = (own_term + partner.astype(jnp.float32)).astype(jnp.bfloat16)
            u = 2 * c + n
            coeffs[u] = updated
            send1[u] = product(blocks[1, n, 1 - bit1], updated).astype(jnp.bfloat16)
            if n == 0:

                @pl.when(c == 0)
                def _():
                    pl.semaphore_wait(barrier, 3)

            @pl.when(is_end)
            def _():
                own_a(u).start()

            @pl.when(is_mid)
            def _():
                own_b(u).start()

    def level(v, u, bit, arrived):
        local_term = product(blocks[v, u % 2, bit], coeffs[u])
        return (local_term + arrived[u].astype(jnp.float32)).astype(jnp.bfloat16)

    def post1(u):
        forward_a(u).wait_recv()
        updated = level(1, u, bit1, recv1)
        coeffs[u] = updated
        send2[u] = product(blocks[2, u % 2, 1 - bit2], updated).astype(jnp.bfloat16)
        second(u).start()

    def post2(u):
        second(u).wait_recv()
        updated = level(2, u, bit2, recv2)
        coeffs[u] = updated
        send3[u] = product(blocks[3, u % 2, 1 - bit3], updated).astype(jnp.bfloat16)
        third(u).start()

    def post3(u):
        third(u).wait_recv()
        result[u] = level(3, u, bit3, recv3)
        for part in range(2):
            store(u, part).start()

    for n in range(2):
        load_maps(n).wait()

    @pl.loop(0, chunks)
    def _(c):
        pre(c)

        @pl.when(jnp.logical_and(is_mid, c > 0))
        def _():
            forward(c - 1)

    for v in range(2, levels):
        load_blocks(v).wait()

    @pl.when(is_mid)
    def _():
        @pl.loop(chunks - 1, units)
        def _(u):
            forward(u)

    @pl.when(is_end)
    def _():
        @pl.loop(0, units)
        def _(u):
            post1(u)

    @pl.loop(0, units + 2)
    def _(u):
        @pl.when(jnp.logical_and(is_mid, u < units))
        def _():
            post1(u)

        @pl.when(jnp.logical_and(u >= 1, u < units + 1))
        def _():
            post2(u - 1)

        @pl.when(u >= 2)
        def _():
            post3(u - 2)

    @pl.loop(0, units)
    def _(u):
        own_a(u).wait_send()
        second(u).wait_send()
        third(u).wait_send()
        for part in range(2):
            store(u, part).wait()

        @pl.when(is_mid)
        def _():
            forward_a(u).wait_send()
            forward_b(u).wait_send()


def local(inputs, leaf_maps, transfer_blocks):
    nodes, _, depth, columns = inputs.shape
    rank = leaf_maps.shape[2]
    levels = transfer_blocks.shape[0]
    chunks = columns // LANES
    units = nodes * chunks
    src_bits = lax.axis_size("src").bit_length() - 1
    tgt_bits = lax.axis_size("tgt").bit_length() - 1
    maps = leaf_maps.reshape(nodes, 2 * rank, depth)
    blocks = transfer_blocks.reshape(levels, nodes, 2, 2 * rank, rank)
    unit = pltpu.VMEM((units, rank, 2 * LANES), jnp.bfloat16)
    dma = pltpu.SemaphoreType.DMA
    return pl.pallas_call(
        functools.partial(kernel, (src_bits, tgt_bits, levels, chunks)),
        out_shape=jax.ShapeDtypeStruct((nodes, 2, rank, columns), jnp.bfloat16),
        in_specs=[pl.BlockSpec(memory_space=pl.ANY)] * 3,
        out_specs=pl.BlockSpec(memory_space=pl.ANY),
        scratch_shapes=[
            pltpu.VMEM((chunks, nodes, depth, 2 * LANES), jnp.bfloat16),
            pltpu.VMEM(maps.shape, jnp.bfloat16),
            pltpu.VMEM(blocks.shape, jnp.bfloat16),
        ]
        + [unit] * 10
        + [
            dma((chunks, nodes, 2)),
            dma((nodes,)),
            dma((levels,)),
            dma((units, 2)),
        ]
        + [dma((units,))] * 10,
        compiler_params=pltpu.CompilerParams(
            collective_id=0, has_side_effects=True, vmem_limit_bytes=60 * 2**20
        ),
    )(inputs, maps, blocks)


def solution(mesh):
    placed = (
        P(("src", "tgt"), None, None, None),
        P(("src", "tgt"), None, None, None),
        P(None, ("src", "tgt"), None, None, None, None),
    )
    return jax.shard_map(
        local,
        mesh=mesh,
        in_specs=placed,
        out_specs=P(("src", "tgt"), None, None, None),
        check_vma=False,
    )
```

time: 129 us -> 75.6 us (0.59)
  waiting for transfers between devices: 86.7 us -> 0 us
  Pallas kernels: 0 us -> 73.2 us
  matrix products: 24.4 us -> 0 us
  starting transfers between devices: 6.21 us -> 0 us
  local copies, waits for them, and re-layouts: 7.26 us -> 2.26 us
  other arithmetic: 4 us -> 0 us
    ppermute x3 -> x0, waiting for transfers between devices: 86.7 us -> none  [partner_2(): return lax.ppermute(block, axis, route)]
    pallas_call x0 -> x1, Pallas kernels: none -> 73.2 us  [local(): pl.pallas_call(functools.partial(kernel, (src_bits, tgt_bits, levels, chu...]
    dot_general x44 -> x0, matrix products: 24.4 us -> none  [batched(): jnp.einsum('nij,njr->nir', left_side, right_side, preferred_element_type=...]
    ppermute x3 -> x0, starting transfers between devices: 6.21 us -> none  [partner_2(): return lax.ppermute(block, axis, route)]
    convert_element_type x3 -> x0, other arithmetic: 2.31 us -> none  [butterfly_level(): (local_term + remote_term(coeffs, other_blocks, axis_src, bit_place)).ast...]
    another operation x4 -> x0, other arithmetic: 1.6 us -> none  [the longest x3 1.3 us: complex_product(): return jnp.stack([real_part, imag_part], axis=1)]
    unnamed x38 -> x1, local copies, waits for them, and re-layouts: 3.6 us -> 2.26 us
    slice x1 -> x0, local copies, waits for them, and re-layouts: 1.32 us -> none  [local(): return butterfly_level(coeffs, transfer_blocks[3], False, tgt_bits - 1)]
  transfers between devices with their start and end apart: 3 -> 0, of which waited for: 3 -> 0; matrix products, arithmetic and copies ran while one was open for 3% -> 0% of each run, Pallas kernels for 0% -> 0%
where the time goes in v1:
time: 75.6 us; the launch traced here: 75.4 us
  Pallas kernels  73.2 us (97%)
  local copies, waits for them, and re-layouts  2.26 us (3%)
    pallas_call x1, Pallas kernels, local(): pl.pallas_call(functools.partial(kernel, (src_bits, tgt_bits, levels, chu...  73.2 us
    unnamed x1, local copies, waits for them, and re-layouts  2.26 us

profile of v1, /device:TPU:0, one launch (start us, length us, event | category | flops | bytes accessed | tf_op | source)
XLA Modules:
  0.0 75.4 jit_solution(9164925618644152126)
XLA Ops:
  0.0 73.2 %shard_map.37 = bf16[2,2,256,512]{3,2,1,0:T(8,128)(2,1)} custom-call(bf16[2,2,1024,512]{3,2,1,0:T(8,128)(2,1)} %inputs.1, bf16[2,512,1024]{2,1,0:T(8,128)(2,1)} %bitcast.3, bf16[4,2,2,512,256]{4,3,2,1,0:T(8,128)(2,1)} %bitcast.2), custom_call_target="tpu_custom_call" | custom-call | tf_op jit(solution)/shard_map/pallas_call | solution.py:265
  73.2 2.3 %copy.5 = bf16[2,2,256,512]{3,2,1,0:T(8,128)(2,1)} copy(bf16[2,2,256,512]{3,2,1,0:T(8,128)(2,1)} %shard_map.37) | data formatting | bytes 2097152
